TPU v7x, 32 devices: a whole 2x2x4 slice. The times are simulated.
32 devices in a mesh: space: 8 (over y, x, core), group: 4 (over z).
Axes of the slice: x: 2, y: 2, z: 4, core: 2. Of those that a mesh axis runs over, the one named last changes fastest.
Arguments:
- snapshot_basis: bfloat16 [65536, 1024], P('space', 'group'), may hold values from -40 to 40
- sketch: float32 [2, 512, 256], replicated, may hold values from -0.25 to 0.25
Outputs:
- merged_basis: bfloat16 [65536, 256], P(('space', 'group'))
All inputs are finite; a program needn't handle non-finite values.
Results may differ from a plain program's by a relative error of at most 0.0067.
Values may be sent and summed in bfloat16 or wider, within the bound.
No kernel may reach another device: no remote copies, remote signals or barrier semaphores. Data moves between devices by JAX's collectives and lax.ppermute only.
A program may use at most 128 MiB of HBM per device.

v0:
```python
import functools

import jax
import jax.numpy as jnp
from jax import lax
from jax.experimental import pallas as pl
from jax.experimental.pallas import tpu as pltpu
from jax.sharding import PartitionSpec as P


STEPS = 5
F32 = jnp.float32
BF16 = jnp.bfloat16


def swap(block, axis, offset):
    count = lax.axis_size(axis)
    return lax.ppermute(block, axis, [(i, i ^ offset) for i in range(count)])


def after(value, *others):
    return lax.optimization_barrier((value,) + others)[0]


def dot_t(a, b):
    return lax.dot_general(a, b, (((0,), (0,)), ((), ())), preferred_element_type=F32)


def dot(a, b):
    return jnp.dot(a, b, preferred_element_type=F32)


def split(x):
    high = x.astype(BF16)
    return high, (x - high.astype(F32)).astype(BF16)


def dot3(a, b):
    ah, al = a
    bh, bl = b
    return dot(ah, bh) + (dot(ah, bl) + dot(al, bh))


def write_slices(me, acc, outs):
    rows = outs[0].shape[0]
    for k, out in enumerate(outs):
        start = pl.multiple_of(jnp.bitwise_xor(me, k) * rows, rows)
        out[...] = acc[pl.ds(start, rows), :]


def own_gram_kernel(ids, x_ref, *refs):
    outs, acc = refs[:-1], refs[-1]
    step = pl.program_id(0)

    @pl.when(step == 0)
    def _():
        acc[...] = jnp.zeros_like(acc)

    x = x_ref[...]
    acc[...] += dot_t(x, x)

    @pl.when(step == pl.num_programs(0) - 1)
    def _():
        write_slices(ids[0], acc, outs)


def own_gram(ids, panel, parts):
    rows, width = panel.shape
    tile = rows // 8
    shape = jax.ShapeDtypeStruct((width // parts, width), F32)
    whole = pl.BlockSpec((width // parts, width), lambda i, ids: (0, 0))
    return pl.pallas_call(
        own_gram_kernel,
        grid_spec=pltpu.PrefetchScalarGridSpec(
            num_scalar_prefetch=1,
            grid=(rows // tile,),
            in_specs=[pl.BlockSpec((tile, width), lambda i, ids: (i, 0))],
            out_specs=[whole] * parts,
            scratch_shapes=[pltpu.VMEM((width, width), F32)],
        ),
        out_shape=[shape] * parts,
        name="own_gram",
    )(ids, panel)


def first_step():
    return (pl.program_id(0) == 0) & (pl.program_id(1) == 0)


def last_step():
    return (pl.program_id(0) == pl.num_programs(0) - 1) & (
        pl.program_id(1) == pl.num_programs(1) - 1
    )


def cross_kernel(sliced, chained, ids, own_ref, other_ref, *refs):
    if chained:
        start, refs = refs[0], refs[1:]
    outs, acc = refs[:-1], refs[-1]

    @pl.when(first_step())
    def _():
        acc[...] = start[...] if chained else jnp.zeros_like(acc)

    width = acc.shape[0]
    own = own_ref[...].reshape(-1, width)
    other = other_ref[...].reshape(-1, width)

    @pl.when(ids[1] == 0)
    def _():
        acc[...] += dot_t(own, other)

    @pl.when(ids[1] == 1)
    def _():
        acc[...] += dot_t(other, own)

    @pl.when(last_step())
    def _():
        if sliced:
            write_slices(ids[0], acc, outs)
        else:
            outs[0][...] = acc[...]


def cross_gram(ids, blocks, other, begin, where, start, parts):
    outer, rows, width = other.shape
    tile = min(rows, blocks.shape[3] // 4)
    shift = begin // tile
    sliced = parts > 0
    chained = start is not None
    count = parts if sliced else 1
    shape = jax.ShapeDtypeStruct((width // count, width), F32)
    whole = pl.BlockSpec((width // count, width), lambda i, r, ids: (0, 0))
    in_specs = [
        pl.BlockSpec(
            (1, 1, 1, tile, width), lambda i, r, ids: (i, ids[where], ids[1], shift + r, 0)
        ),
        pl.BlockSpec((1, tile, width), lambda i, r, ids: (i, r, 0)),
    ]
    args = [blocks, other]
    if chained:
        in_specs.append(pl.BlockSpec((width, width), lambda i, r, ids: (0, 0)))
        args.append(start)
    return pl.pallas_call(
        functools.partial(cross_kernel, sliced, chained),
        grid_spec=pltpu.PrefetchScalarGridSpec(
            num_scalar_prefetch=1,
            grid=(outer, rows // tile),
            in_specs=in_specs,
            out_specs=[whole] * count,
            scratch_shapes=[pltpu.VMEM((width, width), F32)],
        ),
        out_shape=[shape] * count,
        name="cross_gram",
    )(ids, *args)


def assemble_kernel(ids, *refs):
    pieces, out = refs[:-1], refs[-1]
    rows = pieces[0].shape[1]
    for k, piece in enumerate(pieces):
        start = pl.multiple_of(jnp.bitwise_xor(ids[0], k) * rows, rows)
        out[:, pl.ds(start, rows), :] = piece[...]


def assemble(ids, pieces):
    lead, rows, width = pieces[0].shape
    return pl.pallas_call(
        assemble_kernel,
        in_specs=[pl.BlockSpec(memory_space=pltpu.SMEM)]
        + [pl.BlockSpec(memory_space=pltpu.VMEM)] * len(pieces),
        out_specs=pl.BlockSpec(memory_space=pltpu.VMEM),
        out_shape=jax.ShapeDtypeStruct((lead, rows * len(pieces), width), F32),
        name="assemble",
    )(ids, *pieces)


def run_filter(pairs, ids, diag, sketch, pieces, gram, iterate):
    rows, width = pieces[0].shape[1:]
    full = 2 * width
    for p in range(pairs):
        gram[p, :width, :width] = diag[2 * p]
        gram[p, width:, width:] = diag[2 * p + 1]
        for k, piece in enumerate(pieces):
            start = pl.multiple_of(jnp.bitwise_xor(ids[0], k) * rows, rows)
            gram[p, pl.ds(start, rows), width:] = piece[p]
        gram[p, width:, :width] = gram[p, :width, width:].T
    eye = lax.broadcasted_iota(jnp.int32, (full, full), 0) == lax.broadcasted_iota(
        jnp.int32, (full, full), 1
    )
    for p in range(pairs):
        whole = gram[p]
        trace = jnp.sum(jnp.where(eye, whole, 0.0), keepdims=True)
        shifted = whole / (trace / full) - jnp.where(eye, 1.0, 0.0)
        norm = jnp.sqrt(jnp.sum(shifted * shifted, keepdims=True))
        iterate[p] = shifted / (1.0 + norm)

    def step(_, carry):
        xs = [iterate[p] for p in range(pairs)]
        short = [x.astype(BF16) for x in xs]
        squares = [dot(x, x).astype(BF16) for x in short]
        for p in range(pairs):
            iterate[p] = 1.5 * xs[p] - 0.5 * dot(short[p], squares[p])
        return carry

    lax.fori_loop(0, STEPS - 1, step, 0)
    given = sketch[...]
    given_parts = split(given)
    parts = [split(iterate[p]) for p in range(pairs)]
    first = [dot3(part, given_parts) for part in parts]
    second = [dot3(part, split(t)) for part, t in zip(parts, first)]
    third = [dot3(part, split(t)) for part, t in zip(parts, second)]
    mixes = []
    for p in range(pairs):
        applied = 1.5 * first[p] - 0.5 * third[p]
        mixes.append((0.5 * (given + applied)).astype(BF16))
    return mixes


def next_diag(gram, mix):
    gh, gl = split(gram)
    th, tl = split(dot(gh, mix) + dot(gl, mix))
    return dot_t(mix, th) + dot_t(mix, tl)


def pair_filter_kernel(ids, diag, sketch, *refs):
    pieces, (mix_ref, diag_ref, gram, iterate) = refs[:-4], refs[-4:]
    width = diag.shape[-1]
    mixes = run_filter(2, ids, diag, sketch, pieces, gram, iterate)
    for p in range(2):
        mix_ref[p, 0] = mixes[p][:width]
        mix_ref[p, 1] = mixes[p][width:]
        diag_ref[p] = next_diag(gram[p], mixes[p])


def pair_filter(ids, diag, pieces, sketch_level):
    pairs, _, width = pieces[0].shape
    vmem = pl.BlockSpec(memory_space=pltpu.VMEM)
    return pl.pallas_call(
        pair_filter_kernel,
        in_specs=[pl.BlockSpec(memory_space=pltpu.SMEM)] + [vmem] * (2 + len(pieces)),
        out_specs=[vmem] * 2,
        out_shape=[
            jax.ShapeDtypeStruct((pairs, 2, width, width), BF16),
            jax.ShapeDtypeStruct((pairs, width, width), F32),
        ],
        scratch_shapes=[pltpu.VMEM((pairs, 2 * width, 2 * width), F32)] * 2,
        name="pair_filter",
    )(ids, diag, sketch_level, *pieces)


def merge_filter_kernel(which, cuts, ids, diag, sketch, *refs):
    own, others = refs[0], refs[1 : 1 + cuts]
    pieces, (out, diag_ref, mix_ref, gram, iterate) = refs[1 + cuts : -5], refs[-5:]
    width = diag.shape[-1]
    mix = run_filter(1, ids, diag, sketch, pieces, gram, iterate)[0]
    mix_ref[0] = mix[:width]
    mix_ref[1] = mix[width:]
    bit = ids[which]
    begin = 0
    for other in others:
        rows = other.shape[1]
        for h in range(other.shape[0]):
            here = slice(begin, begin + rows)
            total = dot(own[h, here], mix_ref[bit]) + dot(other[h], mix_ref[1 - bit])
            out[h, here] = total.astype(BF16)
        begin += rows
    diag_ref[...] = next_diag(gram[0], mix)


def merge_filter(ids, diag, pieces, sketch_level, which, own, others):
    _, _, width = pieces[0].shape
    vmem = pl.BlockSpec(memory_space=pltpu.VMEM)
    return pl.pallas_call(
        functools.partial(merge_filter_kernel, which, len(others)),
        in_specs=[pl.BlockSpec(memory_space=pltpu.SMEM)]
        + [vmem] * (3 + len(others) + len(pieces)),
        out_specs=[vmem] * 2,
        out_shape=[
            jax.ShapeDtypeStruct(own.shape, BF16),
            jax.ShapeDtypeStruct((width, width), F32),
        ],
        scratch_shapes=[pltpu.VMEM((2, width, width), BF16)]
        + [pltpu.VMEM((1, 2 * width, 2 * width), F32)] * 2,
        name="merge_filter",
    )(ids, diag, sketch_level, own, *others, *pieces)


def merge_own_kernel(ids, own, other, mix, out):
    width = mix.shape[-1]
    bit0, bit1 = ids[1], ids[2]
    a = own[...].reshape(-1, width)
    b = other[...].reshape(-1, width)
    fresh = dot(a, mix[bit1, bit0]) + dot(b, mix[bit1, 1 - bit0])
    out[...] = fresh.astype(BF16).reshape(out.shape)


def merge_own(ids, blocks, other, begin, mix):
    outer, rows, width = other.shape
    tile = min(rows, blocks.shape[3] // 4)
    shift = begin // tile
    part = pl.BlockSpec((1, tile, width), lambda i, r, ids: (i, r, 0))
    return pl.pallas_call(
        merge_own_kernel,
        grid_spec=pltpu.PrefetchScalarGridSpec(
            num_scalar_prefetch=1,
            grid=(outer, rows // tile),
            in_specs=[
                pl.BlockSpec(
                    (1, 1, 1, tile, width), lambda i, r, ids: (i, ids[2], ids[1], shift + r, 0)
                ),
                part,
                pl.BlockSpec(mix.shape, lambda i, r, ids: (0, 0, 0, 0)),
            ],
            out_specs=part,
        ),
        out_shape=jax.ShapeDtypeStruct((outer, rows, width), BF16),
        name="merge_own",
    )(ids, blocks, other, mix)


def merge_other_kernel(chained, ids, out_near, in_near, out_far, in_far, own_merged, mix, *refs):
    if chained:
        start, refs = refs[0], refs[1:]
    merged, outs, acc = refs[0], refs[1:-1], refs[-1]
    bit0, bit1 = ids[1], ids[2]
    pair = 1 - bit1

    @pl.when(first_step())
    def _():
        acc[...] = start[...] if chained else jnp.zeros_like(acc)

    def run(outer_ref, inner_ref):
        fresh = dot(outer_ref[0], mix[pair, pair]) + dot(inner_ref[0], mix[pair, 1 - pair])
        merged[0] = fresh.astype(BF16)

    @pl.when(bit0 != bit1)
    def _():
        run(out_near, in_near)

    @pl.when(bit0 == bit1)
    def _():
        run(out_far, in_far)

    @pl.when(bit1 == 0)
    def _():
        acc[...] += dot_t(own_merged[0], merged[0])

    @pl.when(bit1 == 1)
    def _():
        acc[...] += dot_t(merged[0], own_merged[0])

    @pl.when(last_step())
    def _():
        if len(outs) == 1:
            outs[0][...] = acc[...]
        else:
            write_slices(ids[0], acc, outs)


def merge_other(ids, panels, begins, sizes, own_begin, own_merged, mix, start, parts):
    outer, _, width = own_merged.shape
    rows = sizes
    tile = rows
    while any(b % tile for b in begins + [own_begin]) or tile > 512:
        tile //= 2
    shifts = [b // tile for b in begins + [own_begin]]
    specs = [
        pl.BlockSpec((1, tile, width), functools.partial(lambda s, i, r, ids: (i, s + r, 0), s))
        for s in shifts
    ]
    count = max(parts, 1)
    shape = jax.ShapeDtypeStruct((width // count, width), F32)
    whole = pl.BlockSpec((width // count, width), lambda i, r, ids: (0, 0))
    chained = start is not None
    more = [pl.BlockSpec((width, width), lambda i, r, ids: (0, 0))] if chained else []
    return pl.pallas_call(
        functools.partial(merge_other_kernel, chained),
        grid_spec=pltpu.PrefetchScalarGridSpec(
            num_scalar_prefetch=1,
            grid=(outer, rows // tile),
            in_specs=specs + [pl.BlockSpec(mix.shape, lambda i, r, ids: (0, 0, 0, 0))] + more,
            out_specs=[pl.BlockSpec((1, tile, width), lambda i, r, ids: (i, r, 0))]
            + [whole] * count,
            scratch_shapes=[pltpu.VMEM((width, width), F32)],
        ),
        out_shape=[jax.ShapeDtypeStruct((outer, rows, width), BF16)] + [shape] * count,
        name="merge_other",
    )(ids, *panels, own_merged, mix, *([start] if chained else []))


def scatter_space(pieces):
    total = pieces[0]
    got = [swap(piece, "space", k) for k, piece in enumerate(pieces) if k > 0]
    for piece in got:
        total = total + piece
    return total


def gather_space(piece):
    count = lax.axis_size("space")
    pieces = [piece] + [None] * (count - 1)
    for k in range(2, count, 2):
        pieces[k] = swap(piece, "space", k)
    for k in range(0, count, 2):
        pieces[k + 1] = swap(pieces[k], "space", 1)
    return pieces


def compute(snapshot_basis, sketch):
    rows, width = snapshot_basis.shape
    groups = lax.axis_size("group")
    parts = lax.axis_size("space")
    levels = groups.bit_length() - 1
    member = lax.axis_index("group")
    bit0 = member & 1
    bit1 = member >> 1 & 1
    ids = jnp.stack([lax.axis_index("space"), bit0, bit1, 1 - bit1]).astype(jnp.int32)
    block_rows = rows // groups
    outer = groups // 4
    blocks = snapshot_basis.reshape(outer, 2, 2, block_rows, width)
    cut = block_rows * 3 // 4
    tail = block_rows - cut

    def pick(index1, index0, begin=0, size=block_rows):
        start = (0, index1, index0, begin, 0)
        return lax.dynamic_slice(blocks, start, (outer, 1, 1, size, width)).reshape(
            outer, size, width
        )

    def send(value, routes):
        return lax.ppermute(value, "group", routes)

    middle, forward, rise, leave = [], [], [], []
    for base in range(0, groups, 4):
        middle += [(base + 1, base + 2), (base + 2, base + 1)]
        forward += [(base + 1, base), (base + 2, base + 3)]
        rise += [(base + 1, base + 3), (base + 2, base)]
        leave += [(base, base + 2), (base + 3, base + 1)]
    pair = [(i, i ^ 1) for i in range(groups)]

    far = send(pick(1 - bit1, 1 - bit0), pair)
    pass_on = send(pick(1 - bit1, bit0), middle)

    own_sum = scatter_space(own_gram(ids, snapshot_basis, parts))
    turned = [own_sum] + [swap(own_sum, "group", k) for k in (1, 2, 3)]

    near_head = send(after(pick(bit1, 1 - bit0, 0, cut), own_sum), pair)
    keep = send(after(pick(1 - bit1, 1 - bit0), own_sum), middle)
    near_tail = send(after(pick(bit1, 1 - bit0, cut, tail), own_sum), pair)
    head_rise = send(after(far[:, :cut], own_sum), rise)

    quad = member & 3
    stacked = jnp.stack(turned)
    diag_slices = jnp.stack(
        [lax.dynamic_index_in_dim(stacked, quad ^ g, 0, keepdims=False) for g in range(4)]
    )
    diag = assemble(ids, gather_space(diag_slices))

    half = cross_gram(ids, blocks, far, 0, 3, None, 0)[0]
    half = cross_gram(ids, blocks, near_head, 0, 2, after(half, diag), 0)[0]
    cross_slices = cross_gram(ids, blocks, near_tail, cut, 2, half, parts)
    cross_sum = scatter_space(cross_slices)
    one, two, three = [swap(cross_sum, "group", k) for k in (1, 2, 3)]
    mine = cross_sum + one
    theirs = two + three
    both = jnp.stack([jnp.where(bit1 == 0, mine, theirs), jnp.where(bit1 == 0, theirs, mine)])

    head_leave = send(after(pick(1 - bit1, bit0, 0, cut), both), leave)
    head_pass = send(after(pass_on[:, :cut], both), forward)
    tail_rise = send(after(far[:, cut:], both), rise)
    tail_leave = send(after(pick(1 - bit1, bit0, cut, tail), both), leave)
    tail_pass = send(after(pass_on[:, cut:], both), forward)

    mix, diag = pair_filter(ids, diag, gather_space(both), sketch[0])

    own_head = merge_own(ids, blocks, near_head, 0, mix)
    own_tail = merge_own(ids, blocks, near_tail, cut, mix)
    other_head, half = merge_other(
        ids, [head_leave, keep, head_rise, head_pass], [0] * 4, cut, 0, own_head, mix, None, 0
    )
    results = merge_other(
        ids, [tail_leave, keep, tail_rise, tail_pass], [0, cut, 0, 0], tail, 0, own_tail, mix,
        half, parts,
    )
    other_tail, slices = results[0], results[1:]
    total = scatter_space(slices)
    one, two, three = [swap(total, "group", k) for k in (1, 2, 3)]
    total = (total + one) + (two + three)
    own_merged = jnp.concatenate([own_head, own_tail], axis=1)
    merged, diag_own = merge_filter(
        ids, diag, gather_space(total[None]), sketch[1], 2, own_merged, [other_head, other_tail]
    )

    for level in range(2, levels):
        bit = member >> level & 1
        pairs = merged.reshape(-1, 2, block_rows, width)
        kept = lax.dynamic_index_in_dim(pairs, bit, 1, keepdims=False)
        given = lax.dynamic_index_in_dim(pairs, 1 - bit, 1, keepdims=False)
        got = swap(given, "group", 1 << level)
        diag_got = swap(diag_own, "group", 1 << level)
        lower = jnp.where(bit == 0, kept, got).reshape(-1, width)
        upper = jnp.where(bit == 0, got, kept).reshape(-1, width)
        cross = dot_t(lower, upper).reshape(parts, width // parts, width)
        place = lax.axis_index("space")
        total = scatter_space(
            [lax.dynamic_index_in_dim(cross, place ^ k, 0, keepdims=False) for k in range(parts)],
        )
        for low in range(level + 1):
            total = total + swap(total, "group", 1 << low)
        diag = jnp.stack(
            [jnp.where(bit == 0, diag_own, diag_got), jnp.where(bit == 0, diag_got, diag_own)]
        )
        flag = jnp.stack([lax.axis_index("space"), bit]).astype(jnp.int32)
        merged, diag_own = merge_filter(
            flag, diag, gather_space(total[None]), sketch[level], 1, kept, [got]
        )
    return merged.reshape(block_rows, width)


def solution(mesh):
    in_specs = (P("space", "group"), P())
    out_specs = P(("space", "group"), None)
    return jax.shard_map(compute, mesh=mesh, in_specs=in_specs, out_specs=out_specs, check_vma=False)
```

profile of v0, /device:TPU:0, one launch (start us, length us, event | category | flops | bytes accessed | tf_op | source)
XLA Modules:
  0.0 219.0 jit_solution(8723677788377520452)
XLA Ops:
  0.7 7.5 %own_gram.1 = (f32[32,256]{1,0:T(8,128)}, f32[32,256]{1,0:T(8,128)}, f32[32,256]{1,0:T(8,128)}, f32[32,256]{1,0:T(8,128)}, f32[32,256]{1,0:T(8,128)}, /*index=5*...) custom-call(s32[4]{0:T(128)} %pad_add_fusion.ids, bf16[8192,256]{1,0:T(8,128)(2,1)} %x_ref.1), custom_call_target="tpu_custom_call" | custom-call | tf_op jit(solution)/shard_map/own_gram/pallas_call | solution.py:72
  8.7 2.6 %collective-permute-start.1 = (f32[32,256]{1,0:T(8,128)}, f32[32,256]{1,0:T(8,128)S(1)}, u32[]{:S(2)}, u32[]{:S(2)}) collective-permute-start(f32[32,256]{1,0:T(8,128)} %get-tuple-element.47), channel_id=1, source_target_pairs={{0,8},{4,12},{8,0},{12,4},{16,24},{20,28},{24,16},{28,20},{1,9},{5... | collective-permute-start | bytes 98312 | tf_op jit(solution)/shard_map/ppermute | solution.py:18
  13.1 2.6 %collective-permute-start.5 = (f32[32,256]{1,0:T(8,128)}, f32[32,256]{1,0:T(8,128)S(1)}, u32[]{:S(2)}, u32[]{:S(2)}) collective-permute-start(f32[32,256]{1,0:T(8,128)} %get-tuple-element.51), channel_id=1, source_target_pairs={{0,24},{4,28},{8,16},{12,20},{16,8},{20,12},{24,0},{28,4},{1,25},{... | collective-permute-start | bytes 98312 | tf_op jit(solution)/shard_map/ppermute | solution.py:18
  15.9 3.0 %dynamic-slice_bitcast_fusion = (bf16[1,2048,256]{2,1,0:T(8,128)(2,1)}, bf16[1,2048,256]{2,1,0:T(8,128)(2,1)}) fusion(bf16[1,2,2,2048,256]{4,3,2,1,0:T(8,128)(2,1)} %bitcast.32, s32[]{:T(128)S(6)} %select_n.54, s32[]{:T(128)S(6)} %select_n.57, s32[]{:T(128)S(6)} %select_n.53), kind=kLoop, calls=%fused_computation.1 | loop fusion | bytes 4194316 | tf_op jit(solution)/shard_map/reshape | solution.py:427
  20.5 3.6 %collective-permute-start.19 = (bf16[1,2048,256]{2,1,0:T(8,128)(2,1)}, bf16[1,2048,256]{2,1,0:T(8,128)(2,1)S(1)}, u32[]{:S(2)}, u32[]{:S(2)}) collective-permute-start(bf16[1,2048,256]{2,1,0:T(8,128)(2,1)} %get-tuple-element.67), channel_id=1, source_target_pairs={{0,1},{1,0},{2,3},{3,2},{4,5},{5,4},{6,7},{7,6},{8,9},{9,8},{10,11... | collective-permute-start | bytes 3145736 | tf_op jit(solution)/shard_map/ppermute | solution.py:432
  25.7 2.9 %collective-permute-start.7 = (f32[32,256]{1,0:T(8,128)S(1)}, f32[32,256]{1,0:T(8,128)S(1)}, u32[]{:S(2)}, u32[]{:S(2)}) collective-permute-start(f32[32,256]{1,0:T(8,128)S(1)} %add_add_fusion.2), channel_id=1, source_target_pairs={{0,1},{1,0},{2,3},{3,2},{4,5},{5,4},{6,7},{7,6},{8,9},{9,8},{10,11... | collective-permute-start | bytes 98312 | tf_op jit(solution)/shard_map/ppermute | solution.py:18
  28.6 2.6 %dynamic-slice_bitcast_fusion.2 = (bf16[1,1536,256]{2,1,0:T(8,128)(2,1)}, bf16[1,1536,256]{2,1,0:T(8,128)(2,1)}) fusion(bf16[1,2,2,2048,256]{4,3,2,1,0:T(8,128)(2,1)} %bitcast.33, s32[]{:T(128)S(6)} %select_n.54, s32[]{:T(128)S(6)} %select_n.57, s32[]{:T(128)S(6)} %select_n.52, s32[]{:T(128)S(6)} %select_n.53), kind=kLoop, calls=%fused_computation.3 | loop fusion | bytes 3145744 | tf_op jit(solution)/shard_map/reshape | solution.py:427
  31.2 19.1 %collective-permute-done.9 = f32[32,256]{1,0:T(8,128)S(1)} collective-permute-done((f32[32,256]{1,0:T(8,128)S(1)}, f32[32,256]{1,0:T(8,128)S(1)}, u32[]{:S(2)}, u32[]{:S(2)}) %collective-permute-start.9) | collective-permute-done | bytes 32800 | tf_op jit(solution)/shard_map/ppermute | solution.py:18
  53.3 3.2 %collective-permute-done.15.refs_6_ = f32[4,32,256]{2,1,0:T(8,128)S(1)} collective-permute-done((f32[4,32,256]{2,1,0:T(8,128)S(1)}, f32[4,32,256]{2,1,0:T(8,128)S(1)}, u32[]{:S(2)}, u32[]{:S(2)}) %collective-permute-start.15) | collective-permute-done | bytes 131104 | tf_op jit(solution)/shard_map/ppermute | solution.py:18
  71.3 4.5 %cross_gram.3.refs_0_ = f32[256,256]{1,0:T(8,128)} custom-call(s32[4]{0:T(128)} %pad_add_fusion.ids, bf16[1,2,2,2048,256]{4,3,2,1,0:T(8,128)(2,1)} %bitcast.35, bf16[1,2048,256]{2,1,0:T(8,128)(2,1)} %copy-done.2), custom_call_target="tpu_custom_call" | custom-call | tf_op jit(solution)/shard_map/cross_gram/pallas_call | solution.py:144
  76.7 4.2 %cross_gram.4.refs_0_ = f32[256,256]{1,0:T(8,128)} custom-call(s32[4]{0:T(128)} %pad_add_fusion.ids, bf16[1,2,2,2048,256]{4,3,2,1,0:T(8,128)(2,1)} %bitcast.36, bf16[1,1536,256]{2,1,0:T(8,128)(2,1)} %copy-done.4, f32[256,256]{1,0:T(8,128)} %cross_gram.3.refs_0_), custom_call_target="tpu_custom_call" | custom-call | tf_op jit(solution)/shard_map/cross_gram/pallas_call | solution.py:144
  81.7 2.8 %cross_gram.5 = (f32[32,256]{1,0:T(8,128)}, f32[32,256]{1,0:T(8,128)}, f32[32,256]{1,0:T(8,128)}, f32[32,256]{1,0:T(8,128)}, f32[32,256]{1,0:T(8,128)}, /*index=...) custom-call(s32[4]{0:T(128)} %pad_add_fusion.ids, bf16[1,2,2,2048,256]{4,3,2,1,0:T(8,128)(2,1)} %bitcast.37, ...), custom_call_target="tpu_custom_call" | custom-call | tf_op jit(solution)/shard_map/cross_gram/pallas_call | solution.py:144
  96.6 3.0 %collective-permute-start.29 = (f32[32,256]{1,0:T(8,128)S(1)}, f32[32,256]{1,0:T(8,128)S(1)}, u32[]{:S(2)}, u32[]{:S(2)}) collective-permute-start(f32[32,256]{1,0:T(8,128)S(1)} %add_add_fusion.1), channel_id=1, source_target_pairs={{0,3},{1,2},{2,1},{3,0},{4,7},{5,6},{6,5},{7,4},{8,11},{9,10},{10,... | collective-permute-start | bytes 98312 | tf_op jit(solution)/shard_map/ppermute | solution.py:18
  105.2 6.1 %collective-permute-start.37 = (bf16[1,1536,256]{2,1,0:T(8,128)(2,1)}, bf16[1,1536,256]{2,1,0:T(8,128)(2,1)}, u32[]{:S(2)}, u32[]{:S(2)}) collective-permute-start(bf16[1,1536,256]{2,1,0:T(8,128)(2,1)} %get-tuple-element.66), channel_id=1, source_target_pairs={{0,2},{3,1},{4,6},{7,5},{8,10},{11,9},{12,14},{15,13},{16,18},{19,... | collective-permute-start | bytes 2359304 | tf_op jit(solution)/shard_map/ppermute | solution.py:432
  119.3 2.8 %collective-permute-done.31.refs_2_ = f32[2,32,256]{2,1,0:T(8,128)S(1)} collective-permute-done((f32[2,32,256]{2,1,0:T(8,128)S(1)}, f32[2,32,256]{2,1,0:T(8,128)S(1)}, u32[]{:S(2)}, u32[]{:S(2)}) %collective-permute-start.31) | collective-permute-done | bytes 65568 | tf_op jit(solution)/shard_map/ppermute | solution.py:18
  124.6 6.7 %collective-permute-start.42 = (bf16[1,512,256]{2,1,0:T(8,128)(2,1)}, bf16[1,512,256]{2,1,0:T(8,128)(2,1)S(1)}, u32[]{:S(2)}, u32[]{:S(2)}) collective-permute-start(bf16[1,512,256]{2,1,0:T(8,128)(2,1)} %get-tuple-element.71), channel_id=1, source_target_pairs={{0,2},{3,1},{4,6},{7,5},{8,10},{11,9},{12,14},{15,13},{16,18},{19,... | collective-permute-start | bytes 786440 | tf_op jit(solution)/shard_map/ppermute | solution.py:432
  132.6 14.5 %collective-permute-done.39.out_far = bf16[1,1536,256]{2,1,0:T(8,128)(2,1)S(1)} collective-permute-done((bf16[1,1536,256]{2,1,0:T(8,128)(2,1)S(1)}, bf16[1,1536,256]{2,1,0:T(8,128)(2,1)S(1)}, u32[]{:S(2)}, u32[]{:S(2)}) %collective-permute-start.39) | collective-permute-done | bytes 786464 | tf_op jit(solution)/shard_map/ppermute | solution.py:432
  149.8 13.3 %pair_filter.1 = (bf16[2,2,256,256]{3,2,1,0:T(8,128)(2,1)}, f32[2,256,256]{2,1,0:T(8,128)}) custom-call(s32[4]{0:T(128)} %pad_add_fusion.ids, f32[4,256,256]{2,1,0:T(8,128)} %assemble.1.diag, f32[512,256]{1,0:T(8,128)} %get-tuple-element.92.sketch, f32[2,32,256]{2,1,0:T(8,128)} %copy-done.13, f32[2,32,256]{2,1,0:T(8,128)} %copy-done.24, ...), custom_call_target="tpu_custom_call" | custom-call | tf_op jit(solution)/shard_map/pair_filter/pallas_call | solution.py:239
  163.1 2.9 %merge_own.3.own_merged = bf16[1,512,256]{2,1,0:T(8,128)(2,1)} custom-call(s32[4]{0:T(128)} %pad_add_fusion.ids, bf16[1,2,2,2048,256]{4,3,2,1,0:T(8,128)(2,1)} %bitcast.38, bf16[1,512,256]{2,1,0:T(8,128)(2,1)} %copy-done.7, bf16[2,2,256,256]{3,2,1,0:T(8,128)(2,1)} %get-tuple-element.65.mix), custom_call_target="tpu_custom_call" | custom-call | tf_op jit(solution)/shard_map/merge_own/pallas_call | solution.py:303
  166.0 4.3 %merge_own.2.own_merged = bf16[1,1536,256]{2,1,0:T(8,128)(2,1)} custom-call(s32[4]{0:T(128)} %pad_add_fusion.ids, bf16[1,2,2,2048,256]{4,3,2,1,0:T(8,128)(2,1)} %bitcast.39, bf16[1,1536,256]{2,1,0:T(8,128)(2,1)} %copy-done.4, bf16[2,2,256,256]{3,2,1,0:T(8,128)(2,1)} %get-tuple-element.65.mix), custom_call_target="tpu_custom_call" | custom-call | tf_op jit(solution)/shard_map/merge_own/pallas_call | solution.py:303
  170.4 6.1 %merge_other.2 = (bf16[1,1536,256]{2,1,0:T(8,128)(2,1)}, f32[256,256]{1,0:T(8,128)}) custom-call(s32[4]{0:T(128)} %pad_add_fusion.ids, bf16[1,1536,256]{2,1,0:T(8,128)(2,1)} %collective-permute-done.37.out_near, bf16[1,2048,256]{2,1,0:T(8,128)(2,1)} %copy-done.1, bf16[1,1536,256]{2,1,0:T(8,128)(2,1)} %copy-done.8, ...), custom_call_target="tpu_custom_call" | custom-call | tf_op jit(solution)/shard_map/merge_other/pallas_call | solution.py:377
  177.4 3.8 %merge_other.3 = (bf16[1,512,256]{2,1,0:T(8,128)(2,1)}, f32[32,256]{1,0:T(8,128)}, f32[32,256]{1,0:T(8,128)}, f32[32,256]{1,0:T(8,128)}, f32[32,256]{1,0:T(8,128...) custom-call(s32[4]{0:T(128)} %pad_add_fusion.ids, ...), custom_call_target="tpu_custom_call" | custom-call | tf_op jit(solution)/shard_map/merge_other/pallas_call | solution.py:377
  191.8 2.6 %collective-permute-start.54 = (f32[32,256]{1,0:T(8,128)S(1)}, f32[32,256]{1,0:T(8,128)S(1)}, u32[]{:S(2)}, u32[]{:S(2)}) collective-permute-start(f32[32,256]{1,0:T(8,128)S(1)} %add_add_fusion), channel_id=1, source_target_pairs={{0,3},{1,2},{2,1},{3,0},{4,7},{5,6},{6,5},{7,4},{8,11},{9,10},{10,... | collective-permute-start | bytes 98312 | tf_op jit(solution)/shard_map/ppermute | solution.py:18
  208.0 11.0 %merge_filter.1 = (bf16[1,2048,256]{2,1,0:T(8,128)(2,1)}, f32[256,256]{1,0:T(8,128)}) custom-call(s32[4]{0:T(128)} %pad_add_fusion.ids, f32[2,256,256]{2,1,0:T(8,128)} %get-tuple-element.64.diag, f32[512,256]{1,0:T(8,128)} %get-tuple-element.91.sketch, bf16[1,2048,256]{2,1,0:T(8,128)(2,1)} %pad_maximum_fusion.refs_0_, ...), custom_call_target="tpu_custom_call" | custom-call | tf_op jit(solution)/shard_map/merge_filter/pallas_call | solution.py:274
  (202 shorter events, 82.4 us)
Async XLA Ops:
  8.7 7.0 %collective-permute-start.1 = (f32[32,256]{1,0:T(8,128)}, f32[32,256]{1,0:T(8,128)S(1)}, u32[]{:S(2)}, u32[]{:S(2)}) collective-permute-start(f32[32,256]{1,0:T(8,128)} %get-tuple-element.47), channel_id=1, source_target_pairs={{0,8},{4,12},{8,0},{12,4},{16,24},{20,28},{24,16},{28,20},{1,9},{5... | collective-permute-start | bytes 98312 | tf_op jit(solution)/shard_map/ppermute | solution.py:18
  11.3 7.5 %collective-permute-start.2 = (f32[32,256]{1,0:T(8,128)}, f32[32,256]{1,0:T(8,128)S(1)}, u32[]{:S(2)}, u32[]{:S(2)}) collective-permute-start(f32[32,256]{1,0:T(8,128)} %get-tuple-element.48), channel_id=1, source_target_pairs={{0,12},{4,8},{8,4},{12,0},{16,28},{20,24},{24,20},{28,16},{1,13},{... | collective-permute-start | bytes 98312 | tf_op jit(solution)/shard_map/ppermute | solution.py:18
  11.3 9.1 %collective-permute-start.3 = (f32[32,256]{1,0:T(8,128)}, f32[32,256]{1,0:T(8,128)S(1)}, u32[]{:S(2)}, u32[]{:S(2)}) collective-permute-start(f32[32,256]{1,0:T(8,128)} %get-tuple-element.49), channel_id=1, source_target_pairs={{0,16},{4,20},{8,24},{12,28},{16,0},{20,4},{24,8},{28,12},{1,17},{... | collective-permute-start | bytes 98312 | tf_op jit(solution)/shard_map/ppermute | solution.py:18
  13.1 11.0 %collective-permute-start.4 = (f32[32,256]{1,0:T(8,128)}, f32[32,256]{1,0:T(8,128)S(1)}, u32[]{:S(2)}, u32[]{:S(2)}) collective-permute-start(f32[32,256]{1,0:T(8,128)} %get-tuple-element.50), channel_id=1, source_target_pairs={{0,20},{4,16},{8,28},{12,24},{16,4},{20,0},{24,12},{28,8},{1,21},{... | collective-permute-start | bytes 98312 | tf_op jit(solution)/shard_map/ppermute | solution.py:18
  13.1 11.0 %collective-permute-start.5 = (f32[32,256]{1,0:T(8,128)}, f32[32,256]{1,0:T(8,128)S(1)}, u32[]{:S(2)}, u32[]{:S(2)}) collective-permute-start(f32[32,256]{1,0:T(8,128)} %get-tuple-element.51), channel_id=1, source_target_pairs={{0,24},{4,28},{8,16},{12,20},{16,8},{20,12},{24,0},{28,4},{1,25},{... | collective-permute-start | bytes 98312 | tf_op jit(solution)/shard_map/ppermute | solution.py:18
  15.8 8.4 %collective-permute-start.6 = (f32[32,256]{1,0:T(8,128)}, f32[32,256]{1,0:T(8,128)S(1)}, u32[]{:S(2)}, u32[]{:S(2)}) collective-permute-start(f32[32,256]{1,0:T(8,128)} %get-tuple-element.52), channel_id=1, source_target_pairs={{0,28},{4,24},{8,20},{12,16},{16,12},{20,8},{24,4},{28,0},{1,29},{... | collective-permute-start | bytes 98312 | tf_op jit(solution)/shard_map/ppermute | solution.py:18
  18.8 82.5 %collective-permute-start.40 = (bf16[1,2048,256]{2,1,0:T(8,128)(2,1)}, bf16[1,2048,256]{2,1,0:T(8,128)(2,1)}, u32[]{:S(2)}, u32[]{:S(2)}) collective-permute-start(bf16[1,2048,256]{2,1,0:T(8,128)(2,1)} %get-tuple-element.87), channel_id=1, source_target_pairs={{1,2},{2,1},{5,6},{6,5},{9,10},{10,9},{13,14},{14,13},{17,18},{18,... | collective-permute-start | bytes 3145736 | tf_op jit(solution)/shard_map/ppermute | solution.py:432
  20.5 49.9 %collective-permute-start.19 = (bf16[1,2048,256]{2,1,0:T(8,128)(2,1)}, bf16[1,2048,256]{2,1,0:T(8,128)(2,1)S(1)}, u32[]{:S(2)}, u32[]{:S(2)}) collective-permute-start(bf16[1,2048,256]{2,1,0:T(8,128)(2,1)} %get-tuple-element.67), channel_id=1, source_target_pairs={{0,1},{1,0},{2,3},{3,2},{4,5},{5,4},{6,7},{7,6},{8,9},{9,8},{10,11... | collective-permute-start | bytes 3145736 | tf_op jit(solution)/shard_map/ppermute | solution.py:432
  24.2 26.2 %collective-permute-start.9 = (f32[32,256]{1,0:T(8,128)S(1)}, f32[32,256]{1,0:T(8,128)S(1)}, u32[]{:S(2)}, u32[]{:S(2)}) collective-permute-start(f32[32,256]{1,0:T(8,128)S(1)} %add_add_fusion.2), channel_id=1, source_target_pairs={{0,3},{1,2},{2,1},{3,0},{4,7},{5,6},{6,5},{7,4},{8,11},{9,10},{10,... | collective-permute-start | bytes 98312 | tf_op jit(solution)/shard_map/ppermute | solution.py:18
  25.6 24.9 %collective-permute-start.8 = (f32[32,256]{1,0:T(8,128)S(1)}, f32[32,256]{1,0:T(8,128)S(1)}, u32[]{:S(2)}, u32[]{:S(2)}) collective-permute-start(f32[32,256]{1,0:T(8,128)S(1)} %add_add_fusion.2), channel_id=1, source_target_pairs={{0,2},{1,3},{2,0},{3,1},{4,6},{5,7},{6,4},{7,5},{8,10},{9,11},{10,... | collective-permute-start | bytes 98312 | tf_op jit(solution)/shard_map/ppermute | solution.py:18
  25.7 24.7 %collective-permute-start.7 = (f32[32,256]{1,0:T(8,128)S(1)}, f32[32,256]{1,0:T(8,128)S(1)}, u32[]{:S(2)}, u32[]{:S(2)}) collective-permute-start(f32[32,256]{1,0:T(8,128)S(1)} %add_add_fusion.2), channel_id=1, source_target_pairs={{0,1},{1,0},{2,3},{3,2},{4,5},{5,4},{6,7},{7,6},{8,9},{9,8},{10,11... | collective-permute-start | bytes 98312 | tf_op jit(solution)/shard_map/ppermute | solution.py:18
  50.4 25.4 %collective-permute-start.18 = (bf16[1,1536,256]{2,1,0:T(8,128)(2,1)}, bf16[1,1536,256]{2,1,0:T(8,128)(2,1)S(1)}, u32[]{:S(2)}, u32[]{:S(2)}) collective-permute-start(bf16[1,1536,256]{2,1,0:T(8,128)(2,1)} %get-tuple-element.54), channel_id=1, source_target_pairs={{0,1},{1,0},{2,3},{3,2},{4,5},{5,4},{6,7},{7,6},{8,9},{9,8},{10,11... | collective-permute-start | bytes 2359304 | tf_op jit(solution)/shard_map/ppermute | solution.py:432
  50.5 5.9 %collective-permute-start.15 = (f32[4,32,256]{2,1,0:T(8,128)S(1)}, f32[4,32,256]{2,1,0:T(8,128)S(1)}, u32[]{:S(2)}, u32[]{:S(2)}) collective-permute-start(f32[4,32,256]{2,1,0:T(8,128)S(1)} %pad_maximum_fusion.2.refs_0_), channel_id=1, source_target_pairs={{0,24},{4,28},{8,16},{12,20},{16,8},{20,12},{24,0},{28,4},{1,25},{... | collective-permute-start | bytes 393224 | tf_op jit(solution)/shard_map/ppermute | solution.py:18
  52.8 6.2 %collective-permute-start.13 = (f32[4,32,256]{2,1,0:T(8,128)S(1)}, f32[4,32,256]{2,1,0:T(8,128)S(1)}, u32[]{:S(2)}, u32[]{:S(2)}) collective-permute-start(f32[4,32,256]{2,1,0:T(8,128)S(1)} %pad_maximum_fusion.2.refs_0_), channel_id=1, source_target_pairs={{0,16},{4,20},{8,24},{12,28},{16,0},{20,4},{24,8},{28,12},{1,17},{... | collective-permute-start | bytes 393224 | tf_op jit(solution)/shard_map/ppermute | solution.py:18
  63.7 17.2 %collective-permute-start.17 = (bf16[1,512,256]{2,1,0:T(8,128)(2,1)S(1)}, bf16[1,512,256]{2,1,0:T(8,128)(2,1)S(1)}, u32[]{:S(2)}, u32[]{:S(2)}) collective-permute-start(bf16[1,512,256]{2,1,0:T(8,128)(2,1)S(1)} %get-tuple-element.53), channel_id=1, source_target_pairs={{0,1},{1,0},{2,3},{3,2},{4,5},{5,4},{6,7},{7,6},{8,9},{9,8},{10,11... | collective-permute-start | bytes 786440 | tf_op jit(solution)/shard_map/ppermute | solution.py:432
  67.3 47.2 %collective-permute-start.38 = (bf16[1,2048,256]{2,1,0:T(8,128)(2,1)}, bf16[1,2048,256]{2,1,0:T(8,128)(2,1)S(1)}, u32[]{:S(2)}, u32[]{:S(2)}) collective-permute-start(bf16[1,2048,256]{2,1,0:T(8,128)(2,1)} %get-tuple-element.67), channel_id=1, source_target_pairs={{1,2},{2,1},{5,6},{6,5},{9,10},{10,9},{13,14},{14,13},{17,18},{18,... | collective-permute-start | bytes 3145736 | tf_op jit(solution)/shard_map/ppermute | solution.py:432
  96.6 8.3 %collective-permute-start.29 = (f32[32,256]{1,0:T(8,128)S(1)}, f32[32,256]{1,0:T(8,128)S(1)}, u32[]{:S(2)}, u32[]{:S(2)}) collective-permute-start(f32[32,256]{1,0:T(8,128)S(1)} %add_add_fusion.1), channel_id=1, source_target_pairs={{0,3},{1,2},{2,1},{3,0},{4,7},{5,6},{6,5},{7,4},{8,11},{9,10},{10,... | collective-permute-start | bytes 98312 | tf_op jit(solution)/shard_map/ppermute | solution.py:18
  101.3 45.9 %collective-permute-start.39 = (bf16[1,1536,256]{2,1,0:T(8,128)(2,1)S(1)}, bf16[1,1536,256]{2,1,0:T(8,128)(2,1)S(1)}, u32[]{:S(2)}, u32[]{:S(2)}) collective-permute-start(bf16[1,1536,256]{2,1,0:T(8,128)(2,1)S(1)} %slice.24), channel_id=1, source_target_pairs={{1,3},{2,0},{5,7},{6,4},{9,11},{10,8},{13,15},{14,12},{17,19},{18,... | collective-permute-start | bytes 2359304 | tf_op jit(solution)/shard_map/ppermute | solution.py:432
  105.2 65.1 %collective-permute-start.37 = (bf16[1,1536,256]{2,1,0:T(8,128)(2,1)}, bf16[1,1536,256]{2,1,0:T(8,128)(2,1)}, u32[]{:S(2)}, u32[]{:S(2)}) collective-permute-start(bf16[1,1536,256]{2,1,0:T(8,128)(2,1)} %get-tuple-element.66), channel_id=1, source_target_pairs={{0,2},{3,1},{4,6},{7,5},{8,10},{11,9},{12,14},{15,13},{16,18},{19,... | collective-permute-start | bytes 2359304 | tf_op jit(solution)/shard_map/ppermute | solution.py:432
  111.4 59.0 %collective-permute-start.41 = (bf16[1,1536,256]{2,1,0:T(8,128)(2,1)}, bf16[1,1536,256]{2,1,0:T(8,128)(2,1)}, u32[]{:S(2)}, u32[]{:S(2)}) collective-permute-start(bf16[1,1536,256]{2,1,0:T(8,128)(2,1)} %slice.25), channel_id=1, source_target_pairs={{1,0},{2,3},{5,4},{6,7},{9,8},{10,11},{13,12},{14,15},{17,16},{18,... | collective-permute-start | bytes 2359304 | tf_op jit(solution)/shard_map/ppermute | solution.py:432
  123.4 7.9 %collective-permute-start.32 = (f32[2,32,256]{2,1,0:T(8,128)S(1)}, f32[2,32,256]{2,1,0:T(8,128)S(1)}, u32[]{:S(2)}, u32[]{:S(2)}) collective-permute-start(f32[2,32,256]{2,1,0:T(8,128)S(1)} %collective-permute-done.31.refs_2_), channel_id=1, source_target_pairs={{0,4},{4,0},{8,12},{12,8},{16,20},{20,16},{24,28},{28,24},{1,5},{5... | collective-permute-start | bytes 196616 | tf_op jit(solution)/shard_map/ppermute | solution.py:18
  124.6 51.9 %collective-permute-start.42 = (bf16[1,512,256]{2,1,0:T(8,128)(2,1)}, bf16[1,512,256]{2,1,0:T(8,128)(2,1)S(1)}, u32[]{:S(2)}, u32[]{:S(2)}) collective-permute-start(bf16[1,512,256]{2,1,0:T(8,128)(2,1)} %get-tuple-element.71), channel_id=1, source_target_pairs={{0,2},{3,1},{4,6},{7,5},{8,10},{11,9},{12,14},{15,13},{16,18},{19,... | collective-permute-start | bytes 786440 | tf_op jit(solution)/shard_map/ppermute | solution.py:432
  131.3 45.2 %collective-permute-start.43 = (bf16[1,512,256]{2,1,0:T(8,128)(2,1)S(1)}, bf16[1,512,256]{2,1,0:T(8,128)(2,1)S(1)}, u32[]{:S(2)}, u32[]{:S(2)}) collective-permute-start(bf16[1,512,256]{2,1,0:T(8,128)(2,1)S(1)} %slice.26), channel_id=1, source_target_pairs={{1,3},{2,0},{5,7},{6,4},{9,11},{10,8},{13,15},{14,12},{17,19},{18,... | collective-permute-start | bytes 786440 | tf_op jit(solution)/shard_map/ppermute | solution.py:432
  147.2 29.3 %collective-permute-start.44 = (bf16[1,512,256]{2,1,0:T(8,128)(2,1)S(1)}, bf16[1,512,256]{2,1,0:T(8,128)(2,1)S(1)}, u32[]{:S(2)}, u32[]{:S(2)}) collective-permute-start(bf16[1,512,256]{2,1,0:T(8,128)(2,1)S(1)} %slice.27), channel_id=1, source_target_pairs={{1,0},{2,3},{5,4},{6,7},{9,8},{10,11},{13,12},{14,15},{17,16},{18,... | collective-permute-start | bytes 786440 | tf_op jit(solution)/shard_map/ppermute | solution.py:432
  (74 other events, 654.7 us)
where the time goes:
time: 220 us; the launch traced here: 219 us
  starting transfers between devices  73.5 us (33%)
  Pallas kernels  62.9 us (29%)
  waiting for transfers between devices  62.3 us (28%)
  local copies, waits for them, and re-layouts  16.4 us (7%)
  other arithmetic  3.34 us (2%)
    ppermute x51, waiting for transfers between devices, swap(): return lax.ppermute(block, axis, [(i, i ^ offset) for i in range(count)])  47.8 us
    ppermute x51, starting transfers between devices, swap(): return lax.ppermute(block, axis, [(i, i ^ offset) for i in range(count)])  47.2 us
    ppermute x11, starting transfers between devices, send(): return lax.ppermute(value, 'group', routes)  26.4 us
    ppermute x11, waiting for transfers between devices, send(): return lax.ppermute(value, 'group', routes)  14.6 us
    pallas_call x1, Pallas kernels, pair_filter(): pl.pallas_call(pair_filter_kernel, in_specs=[pl.BlockSpec(memory_space=pl...  13.3 us
    pallas_call x3, Pallas kernels, cross_gram(): pl.pallas_call(functools.partial(cross_kernel, sliced, chained), grid_spe...  11.5 us
    pallas_call x1, Pallas kernels, merge_filter(): pl.pallas_call(functools.partial(merge_filter_kernel, which, len(others))...  11 us
    pallas_call x2, Pallas kernels, merge_other(): pl.pallas_call(functools.partial(merge_other_kernel, chained), grid_spec=...  9.96 us
  transfers between devices with their start and end apart: 62, of which 26 were waited for; matrix products, arithmetic and copies ran while one was open for 6% of the time, Pallas kernels for 19%

commit v1 on v0

--- a/solution.py
+++ b/solution.py
@@ -41,6 +41,10 @@
     return dot(ah, bh) + (dot(ah, bl) + dot(al, bh))
 
 
+def vmem_limit(mib):
+    return pltpu.CompilerParams(vmem_limit_bytes=mib * 2**20)
+
+
 def write_slices(me, acc, outs):
     rows = outs[0].shape[0]
     for k, out in enumerate(outs):
@@ -66,7 +70,7 @@
 
 def own_gram(ids, panel, parts):
     rows, width = panel.shape
-    tile = rows // 8
+    tile = rows // 4
     shape = jax.ShapeDtypeStruct((width // parts, width), F32)
     whole = pl.BlockSpec((width // parts, width), lambda i, ids: (0, 0))
     return pl.pallas_call(
@@ -79,6 +83,7 @@
             scratch_shapes=[pltpu.VMEM((width, width), F32)],
         ),
         out_shape=[shape] * parts,
+        compiler_params=vmem_limit(8),
         name="own_gram",
     )(ids, panel)
 
@@ -151,6 +156,7 @@
             scratch_shapes=[pltpu.VMEM((width, width), F32)],
         ),
         out_shape=[shape] * count,
+        compiler_params=vmem_limit(8),
         name="cross_gram",
     )(ids, *args)
 
@@ -171,6 +177,7 @@
         + [pl.BlockSpec(memory_space=pltpu.VMEM)] * len(pieces),
         out_specs=pl.BlockSpec(memory_space=pltpu.VMEM),
         out_shape=jax.ShapeDtypeStruct((lead, rows * len(pieces), width), F32),
+        compiler_params=vmem_limit(4),
         name="assemble",
     )(ids, *pieces)
 
@@ -245,6 +252,7 @@
             jax.ShapeDtypeStruct((pairs, width, width), F32),
         ],
         scratch_shapes=[pltpu.VMEM((pairs, 2 * width, 2 * width), F32)] * 2,
+        compiler_params=vmem_limit(24),
         name="pair_filter",
     )(ids, diag, sketch_level, *pieces)
 
@@ -282,6 +290,7 @@
         ],
         scratch_shapes=[pltpu.VMEM((2, width, width), BF16)]
         + [pltpu.VMEM((1, 2 * width, 2 * width), F32)] * 2,
+        compiler_params=vmem_limit(24),
         name="merge_filter",
     )(ids, diag, sketch_level, own, *others, *pieces)
 
@@ -315,6 +324,7 @@
             out_specs=part,
         ),
         out_shape=jax.ShapeDtypeStruct((outer, rows, width), BF16),
+        compiler_params=vmem_limit(8),
         name="merge_own",
     )(ids, blocks, other, mix)
 
@@ -385,6 +395,7 @@
             scratch_shapes=[pltpu.VMEM((width, width), F32)],
         ),
         out_shape=[jax.ShapeDtypeStruct((outer, rows, width), BF16)] + [shape] * count,
+        compiler_params=vmem_limit(8),
         name="merge_other",
     )(ids, *panels, own_merged, mix, *([start] if chained else []))
 

time: 220 us -> 190 us (0.86)
  Pallas kernels: 62.9 us -> 35.5 us
  waiting for transfers between devices: 62.3 us -> 69.5 us
  starting transfers between devices: 73.5 us -> 68.6 us
  other arithmetic: 3.34 us -> 0.25 us
    pallas_call x3, Pallas kernels: 11.5 us -> 4.36 us  [cross_gram(): pl.pallas_call(functools.partial(cross_kernel, sliced, chained), grid_spe...]
    pallas_call x2, Pallas kernels: 9.96 us -> 4.26 us  [merge_other(): pl.pallas_call(functools.partial(merge_other_kernel, chained), grid_spec=...]
    ppermute x11, starting transfers between devices: 26.4 us -> 21.1 us  [send(): return lax.ppermute(value, 'group', routes)]
    pallas_call x1, Pallas kernels: 7.52 us -> 2.57 us  [own_gram(): pl.pallas_call(own_gram_kernel, grid_spec=pltpu.PrefetchScalarGridSpec(nu...]
    pallas_call x2, Pallas kernels: 7.21 us -> 2.33 us  [merge_own(): pl.pallas_call(merge_own_kernel, grid_spec=pltpu.PrefetchScalarGridSpec(n...]
    ppermute x51, waiting for transfers between devices: 47.8 us -> 52.3 us  [swap(): return lax.ppermute(block, axis, [(i, i ^ offset) for i in range(count)])]
    ppermute x11, waiting for transfers between devices: 14.6 us -> 17.2 us  [send(): return lax.ppermute(value, 'group', routes)]
    unnamed x72 -> x12, local copies, waits for them, and re-layouts: 4.74 us -> 4.39 us
  transfers between devices with their start and end apart: 62 -> 62, of which waited for: 26 -> 26; matrix products, arithmetic and copies ran while one was open for 6% -> 6% of each run, Pallas kernels for 19% -> 12%
where the time goes in v1:
time: 190 us
  waiting for transfers between devices  69.5 us (37%)
  starting transfers between devices  68.6 us (36%)
  Pallas kernels  35.5 us (19%)
  local copies, waits for them, and re-layouts  15.3 us (8%)
    ppermute x51, waiting for transfers between devices, swap(): return lax.ppermute(block, axis, [(i, i ^ offset) for i in range(count)])  52.3 us
    ppermute x51, starting transfers between devices, swap(): return lax.ppermute(block, axis, [(i, i ^ offset) for i in range(count)])  47.5 us
    ppermute x11, starting transfers between devices, send(): return lax.ppermute(value, 'group', routes)  21.1 us
    ppermute x11, waiting for transfers between devices, send(): return lax.ppermute(value, 'group', routes)  17.2 us
    pallas_call x1, Pallas kernels, pair_filter(): pl.pallas_call(pair_filter_kernel, in_specs=[pl.BlockSpec(memory_space=pl...  11.6 us
    pallas_call x1, Pallas kernels, merge_filter(): pl.pallas_call(functools.partial(merge_filter_kernel, which, len(others))...  9.71 us
    reshape x3, local copies, waits for them, and re-layouts, pick(): lax.dynamic_slice(blocks, start, (outer, 1, 1, size, width))  7.42 us
    unnamed x12, local copies, waits for them, and re-layouts  4.39 us
  transfers between devices with their start and end apart: 62, of which 26 were waited for; matrix products, arithmetic and copies ran while one was open for 6% of the time, Pallas kernels for 12%

profile of v1, /device:TPU:0, one launch (start us, length us, event | category | flops | bytes accessed | tf_op | source)
XLA Modules:
  0.0 189.7 jit_solution(6277294568743718286)
XLA Ops:
  2.3 2.6 %own_gram.1 = (f32[32,256]{1,0:T(8,128)S(1)}, f32[32,256]{1,0:T(8,128)S(1)}, f32[32,256]{1,0:T(8,128)S(1)}, f32[32,256]{1,0:T(8,128)S(1)}, f32[32,256]{1,0:T(8,1...) custom-call(s32[4]{0:T(128)S(1)} %pad_add_fusion.ids, bf16[8192,256]{1,0:T(8,128)(2,1)S(1)} %copy-done), custom_call_target="tpu_custom_call" | custom-call | tf_op jit(solution)/shard_map/own_gram/pallas_call | solution.py:76
  5.4 2.5 %collective-permute-start.1 = (f32[32,256]{1,0:T(8,128)S(1)}, f32[32,256]{1,0:T(8,128)S(1)}, u32[]{:S(2)}, u32[]{:S(2)}) collective-permute-start(f32[32,256]{1,0:T(8,128)S(1)} %get-tuple-element.47), channel_id=1, source_target_pairs={{0,8},{4,12},{8,0},{12,4},{16,24},{20,28},{24,16},{28,20},{1,9},{5... | collective-permute-start | bytes 98312 | tf_op jit(solution)/shard_map/ppermute | solution.py:18
  9.8 2.6 %collective-permute-start.5 = (f32[32,256]{1,0:T(8,128)S(1)}, f32[32,256]{1,0:T(8,128)S(1)}, u32[]{:S(2)}, u32[]{:S(2)}) collective-permute-start(f32[32,256]{1,0:T(8,128)S(1)} %get-tuple-element.51), channel_id=1, source_target_pairs={{0,24},{4,28},{8,16},{12,20},{16,8},{20,12},{24,0},{28,4},{1,25},{... | collective-permute-start | bytes 98312 | tf_op jit(solution)/shard_map/ppermute | solution.py:18
  12.5 3.0 %dynamic-slice_bitcast_fusion = (bf16[1,2048,256]{2,1,0:T(8,128)(2,1)}, bf16[1,2048,256]{2,1,0:T(8,128)(2,1)}) fusion(bf16[1,2,2,2048,256]{4,3,2,1,0:T(8,128)(2,1)} %bitcast.32, s32[]{:T(128)S(6)} %select_n.54, s32[]{:T(128)S(6)} %select_n.57, s32[]{:T(128)S(6)} %select_n.53), kind=kLoop, calls=%fused_computation.1 | loop fusion | bytes 4194316 | tf_op jit(solution)/shard_map/reshape | solution.py:438
  17.2 3.6 %collective-permute-start.19 = (bf16[1,2048,256]{2,1,0:T(8,128)(2,1)}, bf16[1,2048,256]{2,1,0:T(8,128)(2,1)S(1)}, u32[]{:S(2)}, u32[]{:S(2)}) collective-permute-start(bf16[1,2048,256]{2,1,0:T(8,128)(2,1)} %get-tuple-element.67), channel_id=1, source_target_pairs={{0,1},{1,0},{2,3},{3,2},{4,5},{5,4},{6,7},{7,6},{8,9},{9,8},{10,11... | collective-permute-start | bytes 3145736 | tf_op jit(solution)/shard_map/ppermute | solution.py:443
  22.4 2.9 %collective-permute-start.7 = (f32[32,256]{1,0:T(8,128)S(1)}, f32[32,256]{1,0:T(8,128)S(1)}, u32[]{:S(2)}, u32[]{:S(2)}) collective-permute-start(f32[32,256]{1,0:T(8,128)S(1)} %add_add_fusion.2), channel_id=1, source_target_pairs={{0,1},{1,0},{2,3},{3,2},{4,5},{5,4},{6,7},{7,6},{8,9},{9,8},{10,11... | collective-permute-start | bytes 98312 | tf_op jit(solution)/shard_map/ppermute | solution.py:18
  25.3 2.6 %dynamic-slice_bitcast_fusion.2 = (bf16[1,1536,256]{2,1,0:T(8,128)(2,1)}, bf16[1,1536,256]{2,1,0:T(8,128)(2,1)}) fusion(bf16[1,2,2,2048,256]{4,3,2,1,0:T(8,128)(2,1)} %bitcast.33, s32[]{:T(128)S(6)} %select_n.54, s32[]{:T(128)S(6)} %select_n.57, s32[]{:T(128)S(6)} %select_n.52, s32[]{:T(128)S(6)} %select_n.53), kind=kLoop, calls=%fused_computation.3 | loop fusion | bytes 3145744 | tf_op jit(solution)/shard_map/reshape | solution.py:438
  27.9 19.1 %collective-permute-done.9 = f32[32,256]{1,0:T(8,128)S(1)} collective-permute-done((f32[32,256]{1,0:T(8,128)S(1)}, f32[32,256]{1,0:T(8,128)S(1)}, u32[]{:S(2)}, u32[]{:S(2)}) %collective-permute-start.9) | collective-permute-done | bytes 32800 | tf_op jit(solution)/shard_map/ppermute | solution.py:18
  50.0 3.2 %collective-permute-done.15.refs_6_ = f32[4,32,256]{2,1,0:T(8,128)S(1)} collective-permute-done((f32[4,32,256]{2,1,0:T(8,128)S(1)}, f32[4,32,256]{2,1,0:T(8,128)S(1)}, u32[]{:S(2)}, u32[]{:S(2)}) %collective-permute-start.15) | collective-permute-done | bytes 131104 | tf_op jit(solution)/shard_map/ppermute | solution.py:18
  54.9 3.2 %collective-permute-done.11.refs_2_ = f32[4,32,256]{2,1,0:T(8,128)S(1)} collective-permute-done((f32[4,32,256]{2,1,0:T(8,128)S(1)}, f32[4,32,256]{2,1,0:T(8,128)S(1)}, u32[]{:S(2)}, u32[]{:S(2)}) %collective-permute-start.11) | collective-permute-done | bytes 131104 | tf_op jit(solution)/shard_map/ppermute | solution.py:18
  82.8 3.0 %collective-permute-start.29 = (f32[32,256]{1,0:T(8,128)S(1)}, f32[32,256]{1,0:T(8,128)S(1)}, u32[]{:S(2)}, u32[]{:S(2)}) collective-permute-start(f32[32,256]{1,0:T(8,128)S(1)} %add_add_fusion.1), channel_id=1, source_target_pairs={{0,3},{1,2},{2,1},{3,0},{4,7},{5,6},{6,5},{7,4},{8,11},{9,10},{10,... | collective-permute-start | bytes 98312 | tf_op jit(solution)/shard_map/ppermute | solution.py:18
  90.2 3.9 %collective-permute-done.28 = f32[32,256]{1,0:T(8,128)S(1)} collective-permute-done((f32[32,256]{1,0:T(8,128)S(1)}, f32[32,256]{1,0:T(8,128)S(1)}, u32[]{:S(2)}, u32[]{:S(2)}) %collective-permute-start.28) | collective-permute-done | bytes 32800 | tf_op jit(solution)/shard_map/ppermute | solution.py:18
  94.2 2.9 %collective-permute-start.37 = (bf16[1,1536,256]{2,1,0:T(8,128)(2,1)}, bf16[1,1536,256]{2,1,0:T(8,128)(2,1)S(1)}, u32[]{:S(2)}, u32[]{:S(2)}) collective-permute-start(bf16[1,1536,256]{2,1,0:T(8,128)(2,1)} %get-tuple-element.66), channel_id=1, source_target_pairs={{0,2},{3,1},{4,6},{7,5},{8,10},{11,9},{12,14},{15,13},{16,18},{19,... | collective-permute-start | bytes 2359304 | tf_op jit(solution)/shard_map/ppermute | solution.py:443
  98.4 2.9 %collective-permute-start.35 = (f32[2,32,256]{2,1,0:T(8,128)S(1)}, f32[2,32,256]{2,1,0:T(8,128)S(1)}, u32[]{:S(2)}, u32[]{:S(2)}) collective-permute-start(f32[2,32,256]{2,1,0:T(8,128)S(1)} %pad_maximum_fusion.3.refs_0_), channel_id=1, source_target_pairs={{0,24},{4,28},{8,16},{12,20},{16,8},{20,12},{24,0},{28,4},{1,25},{... | collective-permute-start | bytes 196616 | tf_op jit(solution)/shard_map/ppermute | solution.py:18
  101.2 2.4 %collective-permute-done.35.refs_6_ = f32[2,32,256]{2,1,0:T(8,128)S(1)} collective-permute-done((f32[2,32,256]{2,1,0:T(8,128)S(1)}, f32[2,32,256]{2,1,0:T(8,128)S(1)}, u32[]{:S(2)}, u32[]{:S(2)}) %collective-permute-start.35) | collective-permute-done | bytes 65568 | tf_op jit(solution)/shard_map/ppermute | solution.py:18
  105.5 2.4 %collective-permute-done.31.refs_2_ = f32[2,32,256]{2,1,0:T(8,128)S(1)} collective-permute-done((f32[2,32,256]{2,1,0:T(8,128)S(1)}, f32[2,32,256]{2,1,0:T(8,128)S(1)}, u32[]{:S(2)}, u32[]{:S(2)}) %collective-permute-start.31) | collective-permute-done | bytes 65568 | tf_op jit(solution)/shard_map/ppermute | solution.py:18
  110.3 4.7 %collective-permute-start.42 = (bf16[1,512,256]{2,1,0:T(8,128)(2,1)S(1)}, bf16[1,512,256]{2,1,0:T(8,128)(2,1)S(1)}, u32[]{:S(2)}, u32[]{:S(2)}) collective-permute-start(bf16[1,512,256]{2,1,0:T(8,128)(2,1)S(1)} %copy-done.5), channel_id=1, source_target_pairs={{0,2},{3,1},{4,6},{7,5},{8,10},{11,9},{12,14},{15,13},{16,18},{19,... | collective-permute-start | bytes 786440 | tf_op jit(solution)/shard_map/ppermute | solution.py:443
  116.3 17.2 %collective-permute-done.39.out_far = bf16[1,1536,256]{2,1,0:T(8,128)(2,1)S(1)} collective-permute-done((bf16[1,1536,256]{2,1,0:T(8,128)(2,1)S(1)}, bf16[1,1536,256]{2,1,0:T(8,128)(2,1)S(1)}, u32[]{:S(2)}, u32[]{:S(2)}) %collective-permute-start.39) | collective-permute-done | bytes 786464 | tf_op jit(solution)/shard_map/ppermute | solution.py:443
  136.3 11.6 %pair_filter.1 = (bf16[2,2,256,256]{3,2,1,0:T(8,128)(2,1)S(1)}, f32[2,256,256]{2,1,0:T(8,128)S(1)}) custom-call(s32[4]{0:T(128)S(1)} %pad_add_fusion.ids, f32[4,256,256]{2,1,0:T(8,128)S(1)} %assemble.1.diag, f32[512,256]{1,0:T(8,128)S(1)} %get-tuple-element.92.sketch, f32[2,32,256]{2,1,0:T(8,128)S(1)} %pad_maximum_fusion.3.refs_0_, ...), custom_call_target="tpu_custom_call" | custom-call | tf_op jit(solution)/shard_map/pair_filter/pallas_call | solution.py:246
  150.3 2.9 %merge_other.2 = (bf16[1,1536,256]{2,1,0:T(8,128)(2,1)S(1)}, f32[256,256]{1,0:T(8,128)S(1)}) custom-call(s32[4]{0:T(128)S(1)} %pad_add_fusion.ids, bf16[1,1536,256]{2,1,0:T(8,128)(2,1)S(1)} %collective-permute-done.37.out_near, bf16[1,2048,256]{2,1,0:T(8,128)(2,1)S(1)} %collective-permute-done.38.in_near, ...), custom_call_target="tpu_custom_call" | custom-call | tf_op jit(solution)/shard_map/merge_other/pallas_call | solution.py:387
  158.3 2.5 %collective-permute-start.50 = (f32[32,256]{1,0:T(8,128)S(1)}, f32[32,256]{1,0:T(8,128)S(1)}, u32[]{:S(2)}, u32[]{:S(2)}) collective-permute-start(f32[32,256]{1,0:T(8,128)S(1)} %get-tuple-element.82), channel_id=1, source_target_pairs={{0,24},{4,28},{8,16},{12,20},{16,8},{20,12},{24,0},{28,4},{1,25},{... | collective-permute-start | bytes 98312 | tf_op jit(solution)/shard_map/ppermute | solution.py:18
  165.0 2.9 %collective-permute-start.54 = (f32[32,256]{1,0:T(8,128)S(1)}, f32[32,256]{1,0:T(8,128)S(1)}, u32[]{:S(2)}, u32[]{:S(2)}) collective-permute-start(f32[32,256]{1,0:T(8,128)S(1)} %add_add_fusion), channel_id=1, source_target_pairs={{0,3},{1,2},{2,1},{3,0},{4,7},{5,6},{6,5},{7,4},{8,11},{9,10},{10,... | collective-permute-start | bytes 98312 | tf_op jit(solution)/shard_map/ppermute | solution.py:18
  170.8 2.3 %collective-permute-done.53 = f32[32,256]{1,0:T(8,128)S(1)} collective-permute-done((f32[32,256]{1,0:T(8,128)S(1)}, f32[32,256]{1,0:T(8,128)S(1)}, u32[]{:S(2)}, u32[]{:S(2)}) %collective-permute-start.53) | collective-permute-done | bytes 32800 | tf_op jit(solution)/shard_map/ppermute | solution.py:18
  179.9 9.7 %merge_filter.1 = (bf16[1,2048,256]{2,1,0:T(8,128)(2,1)}, f32[256,256]{1,0:T(8,128)}) custom-call(s32[4]{0:T(128)S(1)} %pad_add_fusion.ids, f32[2,256,256]{2,1,0:T(8,128)S(1)} %get-tuple-element.64.diag, f32[512,256]{1,0:T(8,128)S(1)} %get-tuple-element.91.sketch, bf16[1,2048,256]{2,1,0:T(8,128)(2,1)S(1)} %pad_maximum_fusion.refs_0_, ...), custom_call_target="tpu_custom_call" | custom-call | tf_op jit(solution)/shard_map/merge_filter/pallas_call | solution.py:282
  (142 shorter events, 72.5 us)
Async XLA Ops:
  5.4 7.0 %collective-permute-start.1 = (f32[32,256]{1,0:T(8,128)S(1)}, f32[32,256]{1,0:T(8,128)S(1)}, u32[]{:S(2)}, u32[]{:S(2)}) collective-permute-start(f32[32,256]{1,0:T(8,128)S(1)} %get-tuple-element.47), channel_id=1, source_target_pairs={{0,8},{4,12},{8,0},{12,4},{16,24},{20,28},{24,16},{28,20},{1,9},{5... | collective-permute-start | bytes 98312 | tf_op jit(solution)/shard_map/ppermute | solution.py:18
  8.0 7.6 %collective-permute-start.2 = (f32[32,256]{1,0:T(8,128)S(1)}, f32[32,256]{1,0:T(8,128)S(1)}, u32[]{:S(2)}, u32[]{:S(2)}) collective-permute-start(f32[32,256]{1,0:T(8,128)S(1)} %get-tuple-element.48), channel_id=1, source_target_pairs={{0,12},{4,8},{8,4},{12,0},{16,28},{20,24},{24,20},{28,16},{1,13},{... | collective-permute-start | bytes 98312 | tf_op jit(solution)/shard_map/ppermute | solution.py:18
  8.0 9.2 %collective-permute-start.3 = (f32[32,256]{1,0:T(8,128)S(1)}, f32[32,256]{1,0:T(8,128)S(1)}, u32[]{:S(2)}, u32[]{:S(2)}) collective-permute-start(f32[32,256]{1,0:T(8,128)S(1)} %get-tuple-element.49), channel_id=1, source_target_pairs={{0,16},{4,20},{8,24},{12,28},{16,0},{20,4},{24,8},{28,12},{1,17},{... | collective-permute-start | bytes 98312 | tf_op jit(solution)/shard_map/ppermute | solution.py:18
  9.8 11.0 %collective-permute-start.4 = (f32[32,256]{1,0:T(8,128)S(1)}, f32[32,256]{1,0:T(8,128)S(1)}, u32[]{:S(2)}, u32[]{:S(2)}) collective-permute-start(f32[32,256]{1,0:T(8,128)S(1)} %get-tuple-element.50), channel_id=1, source_target_pairs={{0,20},{4,16},{8,28},{12,24},{16,4},{20,0},{24,12},{28,8},{1,21},{... | collective-permute-start | bytes 98312 | tf_op jit(solution)/shard_map/ppermute | solution.py:18
  9.8 11.0 %collective-permute-start.5 = (f32[32,256]{1,0:T(8,128)S(1)}, f32[32,256]{1,0:T(8,128)S(1)}, u32[]{:S(2)}, u32[]{:S(2)}) collective-permute-start(f32[32,256]{1,0:T(8,128)S(1)} %get-tuple-element.51), channel_id=1, source_target_pairs={{0,24},{4,28},{8,16},{12,20},{16,8},{20,12},{24,0},{28,4},{1,25},{... | collective-permute-start | bytes 98312 | tf_op jit(solution)/shard_map/ppermute | solution.py:18
  12.4 8.4 %collective-permute-start.6 = (f32[32,256]{1,0:T(8,128)S(1)}, f32[32,256]{1,0:T(8,128)S(1)}, u32[]{:S(2)}, u32[]{:S(2)}) collective-permute-start(f32[32,256]{1,0:T(8,128)S(1)} %get-tuple-element.52), channel_id=1, source_target_pairs={{0,28},{4,24},{8,20},{12,16},{16,12},{20,8},{24,4},{28,0},{1,29},{... | collective-permute-start | bytes 98312 | tf_op jit(solution)/shard_map/ppermute | solution.py:18
  15.5 71.9 %collective-permute-start.40 = (bf16[1,2048,256]{2,1,0:T(8,128)(2,1)}, bf16[1,2048,256]{2,1,0:T(8,128)(2,1)}, u32[]{:S(2)}, u32[]{:S(2)}) collective-permute-start(bf16[1,2048,256]{2,1,0:T(8,128)(2,1)} %get-tuple-element.87), channel_id=1, source_target_pairs={{1,2},{2,1},{5,6},{6,5},{9,10},{10,9},{13,14},{14,13},{17,18},{18,... | collective-permute-start | bytes 3145736 | tf_op jit(solution)/shard_map/ppermute | solution.py:443
  17.2 48.0 %collective-permute-start.19 = (bf16[1,2048,256]{2,1,0:T(8,128)(2,1)}, bf16[1,2048,256]{2,1,0:T(8,128)(2,1)S(1)}, u32[]{:S(2)}, u32[]{:S(2)}) collective-permute-start(bf16[1,2048,256]{2,1,0:T(8,128)(2,1)} %get-tuple-element.67), channel_id=1, source_target_pairs={{0,1},{1,0},{2,3},{3,2},{4,5},{5,4},{6,7},{7,6},{8,9},{9,8},{10,11... | collective-permute-start | bytes 3145736 | tf_op jit(solution)/shard_map/ppermute | solution.py:443
  20.8 26.2 %collective-permute-start.9 = (f32[32,256]{1,0:T(8,128)S(1)}, f32[32,256]{1,0:T(8,128)S(1)}, u32[]{:S(2)}, u32[]{:S(2)}) collective-permute-start(f32[32,256]{1,0:T(8,128)S(1)} %add_add_fusion.2), channel_id=1, source_target_pairs={{0,3},{1,2},{2,1},{3,0},{4,7},{5,6},{6,5},{7,4},{8,11},{9,10},{10,... | collective-permute-start | bytes 98312 | tf_op jit(solution)/shard_map/ppermute | solution.py:18
  22.3 24.8 %collective-permute-start.8 = (f32[32,256]{1,0:T(8,128)S(1)}, f32[32,256]{1,0:T(8,128)S(1)}, u32[]{:S(2)}, u32[]{:S(2)}) collective-permute-start(f32[32,256]{1,0:T(8,128)S(1)} %add_add_fusion.2), channel_id=1, source_target_pairs={{0,2},{1,3},{2,0},{3,1},{4,6},{5,7},{6,4},{7,5},{8,10},{9,11},{10,... | collective-permute-start | bytes 98312 | tf_op jit(solution)/shard_map/ppermute | solution.py:18
  22.4 24.7 %collective-permute-start.7 = (f32[32,256]{1,0:T(8,128)S(1)}, f32[32,256]{1,0:T(8,128)S(1)}, u32[]{:S(2)}, u32[]{:S(2)}) collective-permute-start(f32[32,256]{1,0:T(8,128)S(1)} %add_add_fusion.2), channel_id=1, source_target_pairs={{0,1},{1,0},{2,3},{3,2},{4,5},{5,4},{6,7},{7,6},{8,9},{9,8},{10,11... | collective-permute-start | bytes 98312 | tf_op jit(solution)/shard_map/ppermute | solution.py:18
  47.1 22.2 %collective-permute-start.18 = (bf16[1,1536,256]{2,1,0:T(8,128)(2,1)}, bf16[1,1536,256]{2,1,0:T(8,128)(2,1)S(1)}, u32[]{:S(2)}, u32[]{:S(2)}) collective-permute-start(bf16[1,1536,256]{2,1,0:T(8,128)(2,1)} %get-tuple-element.54), channel_id=1, source_target_pairs={{0,1},{1,0},{2,3},{3,2},{4,5},{5,4},{6,7},{7,6},{8,9},{9,8},{10,11... | collective-permute-start | bytes 2359304 | tf_op jit(solution)/shard_map/ppermute | solution.py:443
  60.5 10.4 %collective-permute-start.17 = (bf16[1,512,256]{2,1,0:T(8,128)(2,1)S(1)}, bf16[1,512,256]{2,1,0:T(8,128)(2,1)S(1)}, u32[]{:S(2)}, u32[]{:S(2)}) collective-permute-start(bf16[1,512,256]{2,1,0:T(8,128)(2,1)S(1)} %get-tuple-element.53), channel_id=1, source_target_pairs={{0,1},{1,0},{2,3},{3,2},{4,5},{5,4},{6,7},{7,6},{8,9},{9,8},{10,11... | collective-permute-start | bytes 786440 | tf_op jit(solution)/shard_map/ppermute | solution.py:443
  63.8 37.4 %collective-permute-start.38 = (bf16[1,2048,256]{2,1,0:T(8,128)(2,1)}, bf16[1,2048,256]{2,1,0:T(8,128)(2,1)S(1)}, u32[]{:S(2)}, u32[]{:S(2)}) collective-permute-start(bf16[1,2048,256]{2,1,0:T(8,128)(2,1)} %get-tuple-element.67), channel_id=1, source_target_pairs={{1,2},{2,1},{5,6},{6,5},{9,10},{10,9},{13,14},{14,13},{17,18},{18,... | collective-permute-start | bytes 3145736 | tf_op jit(solution)/shard_map/ppermute | solution.py:443
  82.8 7.4 %collective-permute-start.29 = (f32[32,256]{1,0:T(8,128)S(1)}, f32[32,256]{1,0:T(8,128)S(1)}, u32[]{:S(2)}, u32[]{:S(2)}) collective-permute-start(f32[32,256]{1,0:T(8,128)S(1)} %add_add_fusion.1), channel_id=1, source_target_pairs={{0,3},{1,2},{2,1},{3,0},{4,7},{5,6},{6,5},{7,4},{8,11},{9,10},{10,... | collective-permute-start | bytes 98312 | tf_op jit(solution)/shard_map/ppermute | solution.py:18
  85.8 8.4 %collective-permute-start.28 = (f32[32,256]{1,0:T(8,128)S(1)}, f32[32,256]{1,0:T(8,128)S(1)}, u32[]{:S(2)}, u32[]{:S(2)}) collective-permute-start(f32[32,256]{1,0:T(8,128)S(1)} %add_add_fusion.1), channel_id=1, source_target_pairs={{0,2},{1,3},{2,0},{3,1},{4,6},{5,7},{6,4},{7,5},{8,10},{9,11},{10,... | collective-permute-start | bytes 98312 | tf_op jit(solution)/shard_map/ppermute | solution.py:18
  87.4 6.8 %collective-permute-start.27 = (f32[32,256]{1,0:T(8,128)S(1)}, f32[32,256]{1,0:T(8,128)S(1)}, u32[]{:S(2)}, u32[]{:S(2)}) collective-permute-start(f32[32,256]{1,0:T(8,128)S(1)} %add_add_fusion.1), channel_id=1, source_target_pairs={{0,1},{1,0},{2,3},{3,2},{4,5},{5,4},{6,7},{7,6},{8,9},{9,8},{10,11... | collective-permute-start | bytes 98312 | tf_op jit(solution)/shard_map/ppermute | solution.py:18
  87.5 46.1 %collective-permute-start.39 = (bf16[1,1536,256]{2,1,0:T(8,128)(2,1)S(1)}, bf16[1,1536,256]{2,1,0:T(8,128)(2,1)S(1)}, u32[]{:S(2)}, u32[]{:S(2)}) collective-permute-start(bf16[1,1536,256]{2,1,0:T(8,128)(2,1)S(1)} %slice.24), channel_id=1, source_target_pairs={{1,3},{2,0},{5,7},{6,4},{9,11},{10,8},{13,15},{14,12},{17,19},{18,... | collective-permute-start | bytes 2359304 | tf_op jit(solution)/shard_map/ppermute | solution.py:443
  94.2 56.1 %collective-permute-start.37 = (bf16[1,1536,256]{2,1,0:T(8,128)(2,1)}, bf16[1,1536,256]{2,1,0:T(8,128)(2,1)S(1)}, u32[]{:S(2)}, u32[]{:S(2)}) collective-permute-start(bf16[1,1536,256]{2,1,0:T(8,128)(2,1)} %get-tuple-element.66), channel_id=1, source_target_pairs={{0,2},{3,1},{4,6},{7,5},{8,10},{11,9},{12,14},{15,13},{16,18},{19,... | collective-permute-start | bytes 2359304 | tf_op jit(solution)/shard_map/ppermute | solution.py:443
  97.1 53.2 %collective-permute-start.41 = (bf16[1,1536,256]{2,1,0:T(8,128)(2,1)S(1)}, bf16[1,1536,256]{2,1,0:T(8,128)(2,1)S(1)}, u32[]{:S(2)}, u32[]{:S(2)}) collective-permute-start(bf16[1,1536,256]{2,1,0:T(8,128)(2,1)S(1)} %slice.25), channel_id=1, source_target_pairs={{1,0},{2,3},{5,4},{6,7},{9,8},{10,11},{13,12},{14,15},{17,16},{18,... | collective-permute-start | bytes 2359304 | tf_op jit(solution)/shard_map/ppermute | solution.py:443
  110.3 42.9 %collective-permute-start.42 = (bf16[1,512,256]{2,1,0:T(8,128)(2,1)S(1)}, bf16[1,512,256]{2,1,0:T(8,128)(2,1)S(1)}, u32[]{:S(2)}, u32[]{:S(2)}) collective-permute-start(bf16[1,512,256]{2,1,0:T(8,128)(2,1)S(1)} %copy-done.5), channel_id=1, source_target_pairs={{0,2},{3,1},{4,6},{7,5},{8,10},{11,9},{12,14},{15,13},{16,18},{19,... | collective-permute-start | bytes 786440 | tf_op jit(solution)/shard_map/ppermute | solution.py:443
  115.0 38.2 %collective-permute-start.43 = (bf16[1,512,256]{2,1,0:T(8,128)(2,1)S(1)}, bf16[1,512,256]{2,1,0:T(8,128)(2,1)S(1)}, u32[]{:S(2)}, u32[]{:S(2)}) collective-permute-start(bf16[1,512,256]{2,1,0:T(8,128)(2,1)S(1)} %slice.26), channel_id=1, source_target_pairs={{1,3},{2,0},{5,7},{6,4},{9,11},{10,8},{13,15},{14,12},{17,19},{18,... | collective-permute-start | bytes 786440 | tf_op jit(solution)/shard_map/ppermute | solution.py:443
  133.5 19.7 %collective-permute-start.44 = (bf16[1,512,256]{2,1,0:T(8,128)(2,1)S(1)}, bf16[1,512,256]{2,1,0:T(8,128)(2,1)S(1)}, u32[]{:S(2)}, u32[]{:S(2)}) collective-permute-start(bf16[1,512,256]{2,1,0:T(8,128)(2,1)S(1)} %slice.27), channel_id=1, source_target_pairs={{1,0},{2,3},{5,4},{6,7},{9,8},{10,11},{13,12},{14,15},{17,16},{18,... | collective-permute-start | bytes 786440 | tf_op jit(solution)/shard_map/ppermute | solution.py:443
  154.7 6.1 %collective-permute-start.46 = (f32[32,256]{1,0:T(8,128)S(1)}, f32[32,256]{1,0:T(8,128)S(1)}, u32[]{:S(2)}, u32[]{:S(2)}) collective-permute-start(f32[32,256]{1,0:T(8,128)S(1)} %get-tuple-element.78), channel_id=1, source_target_pairs={{0,8},{4,12},{8,0},{12,4},{16,24},{20,28},{24,16},{28,20},{1,9},{5... | collective-permute-start | bytes 98312 | tf_op jit(solution)/shard_map/ppermute | solution.py:18
  (44 other events, 247.8 us)
